TPU v7x, 512 devices: a whole 4x4x16 slice. The times are simulated.
512 devices in a mesh: row: 16 (over x, z_hi), col: 32 (over z_lo, y, core).
Axes of the slice: x: 4, y: 4, z: 16 (z_hi: 4, z_lo: 4; z = z_hi * 4 + z_lo), core: 2. Of those that a mesh axis runs over, the one named last changes fastest.
Arguments:
- inverse_pool: bfloat16 [16384, 16384], P('row', 'col'), as said below
- factor_one: bfloat16 [16384, 256], P(('row', 'col')), may hold values from -0.046875 to 0.046875
- factor_two: bfloat16 [16384, 256], P(('row', 'col')), may hold values from -0.046875 to 0.046875
- diag_inv_one: float32 [256, 256], replicated, may hold values from -3 to 3
- diag_inv_two: float32 [256, 256], replicated, may hold values from -3 to 3
- struct_one: int32 [64], replicated, may hold values 0 or 1
- struct_two: int32 [64], replicated, may hold values 0 or 1
Outputs:
- column_one: bfloat16 [16384, 256], P(('row', 'col'))
- column_two: bfloat16 [16384, 256], P(('row', 'col'))
- diagonal_one: float32 [256, 256], replicated
- diagonal_two: float32 [256, 256], replicated
Inputs may be any that keep to these rules, and one draw needn't show every extreme that they name: inverse_pool is symmetric: entry (i, j) equals entry (j, i).
All inputs are finite; a program needn't handle non-finite values.
Results may differ from a plain program's by a relative error of at most 0.0007.
Values may be sent and summed in bfloat16 or wider, within the bound.
No kernel may reach another device: no remote copies, remote signals or barrier semaphores. Data moves between devices by JAX's collectives and lax.ppermute only.
A program may use at most 64 MiB of HBM per device.

v0:
```python
import jax
import jax.numpy as jnp
from jax import lax
from jax.sharding import PartitionSpec as P

B = 256


def broadcast(block, axis, owner):
    block = jnp.where(lax.axis_index(axis) == owner, block, jnp.zeros_like(block))
    return lax.psum(block, axis)


def local_mask(struct, first_row, row_count):
    spread = jnp.repeat(struct, B)
    return lax.dynamic_slice_in_dim(spread, first_row, row_count, 0)


def per_device(
    inverse_pool, factor_one, factor_two, diag_inv_one, diag_inv_two, struct_one, struct_two
):
    num_row = lax.axis_size("row")
    num_col = lax.axis_size("col")
    row_count = factor_one.shape[0]
    width = factor_one.shape[1]
    col_width = inverse_pool.shape[1]
    linear = lax.axis_index("row") * num_col + lax.axis_index("col")
    first_row = linear * row_count
    mask_one = local_mask(struct_one, first_row, row_count)
    mask_two = local_mask(struct_two, first_row, row_count)
    masked_one = factor_one * mask_one.astype(jnp.bfloat16)[:, None]
    masked_two = factor_two * mask_two.astype(jnp.bfloat16)[:, None]
    strip_one, strip_two = (
        lax.all_gather(masked_one, "col", axis=0, tiled=True),
        lax.all_gather(masked_two, "col", axis=0, tiled=True),
    )
    stacked = jnp.concatenate([strip_one, strip_two], axis=1)
    col_ratio = num_col // num_row
    root_row = lax.axis_index("col") // col_ratio
    offset = lax.axis_index("col") % col_ratio * col_width
    arrived = broadcast(stacked, "row", root_row)
    owned_rows = lax.dynamic_slice_in_dim(arrived, offset, col_width, 0)
    product = lax.psum_scatter(
        jnp.dot(inverse_pool, owned_rows, preferred_element_type=jnp.float32),
        "col",
        scatter_dimension=0,
        tiled=True,
    )
    product_one = product[:, :width]
    product_two = product[:, width:]
    column_one = (-(product_one * mask_one.astype(jnp.float32)[:, None])).astype(jnp.bfloat16)
    column_two = (-(product_two * mask_two.astype(jnp.float32)[:, None])).astype(jnp.bfloat16)
    term_one = jnp.dot(
        masked_one.astype(jnp.float32).T,
        product_one,
        precision=lax.Precision.HIGHEST,
        preferred_element_type=jnp.float32,
    )
    term_two = jnp.dot(
        masked_two.astype(jnp.float32).T,
        product_two,
        precision=lax.Precision.HIGHEST,
        preferred_element_type=jnp.float32,
    )
    total_one, total_two = lax.psum((term_one, term_two), ("row", "col"))
    return (column_one, column_two, diag_inv_one + total_one, diag_inv_two + total_two)


def solution(mesh):
    in_specs = (
        P("row", "col"),
        P(("row", "col"), None),
        P(("row", "col"), None),
        P(),
        P(),
        P(),
        P(),
    )
    out_specs = (P(("row", "col"), None), P(("row", "col"), None), P(), P())
    return jax.shard_map(
        per_device, mesh=mesh, in_specs=in_specs, out_specs=out_specs, check_vma=False
    )
```

profile of v0, /device:TPU:2, one launch (start us, length us, event | category | flops | bytes accessed | tf_op | source)
XLA Modules:
  0.0 932.4 jit_solution(10251943174924167101)
XLA Ops:
  7.2 0.8 broadcast_bitcast_fusion.1
  8.1 0.7 broadcast_bitcast_fusion
  8.9 0.1 dynamic-slice_convert_fusion
  8.9 0.8 broadcast_multiply_fusion.1
  9.7 46.0 %all_gather.6 = bf16[1024,256]{1,0:T(8,128)(2,1)S(1)} all-gather(bf16[32,256]{1,0:T(8,128)(2,1)S(1)} %broadcast_multiply_fusion.1), channel_id=1, replica_groups=mesh['row'=16,'col'=32] {'col'}, dimensions={0}, use_global_device_ids=true | all-gather | bytes 540672 | tf_op jit(solution)/shard_map/all_gather | solution.py:34
  55.7 0.8 broadcast_multiply_fusion
  56.5 39.3 %all_gather.7 = bf16[1024,256]{1,0:T(8,128)(2,1)S(1)} all-gather(bf16[32,256]{1,0:T(8,128)(2,1)S(1)} %broadcast_multiply_fusion), channel_id=1, replica_groups=mesh['row'=16,'col'=32] {'col'}, dimensions={0}, use_global_device_ids=true | all-gather | bytes 540672 | tf_op jit(solution)/shard_map/all_gather | solution.py:35
  95.8 1.2 maximum_select_fusion
  97.1 0.0 reduce-scatter.4.cloned.1.call-start
  97.1 211.4 %all-reduce.4.cloned.1.call-done = bf16[1024,512]{1,0:T(8,128)(2,1)} async-done(((bf16[1024,512]{1,0:T(8,128)(2,1)}), bf16[1024,512]{1,0:T(8,128)(2,1)}) %all-reduce.4.cloned.1.call-update) | async-done | bytes 1048592 | tf_op jit(solution)/shard_map/psum | solution.py:11
  308.6 1.8 convolution_bitcast_fusion
  310.4 1.9 copy.15
  312.3 0.0 all-reduce.6.cloned.1.call-start
  312.3 148.2 %reduce-scatter.4.cloned.1.call-done = f32[32,512]{1,0:T(8,128)} async-done(((f32[1024,512]{1,0:T(8,128)}), f32[32,512]{1,0:T(8,128)}) %reduce-scatter.4.cloned.1.call-update) | async-done | bytes 65552
  460.5 0.8 fusion.6
  461.3 0.1 copy.18
  461.4 1.8 fusion.2
  463.1 1.8 fusion.4
  465.0 0.7 copy.14
  465.7 0.1 copy.17
  465.8 0.7 copy.13
  466.5 456.0 %all-reduce.6.cloned.1.call-done = (f32[256,256]{1,0:T(8,128)}, f32[256,256]{1,0:T(8,128)}) async-done(((f32[256,256]{1,0:T(8,128)}, f32[256,256]{1,0:T(8,128)}), (f32[256,256]{1,0:T(8,128)}, f32[256,256]{1,0:T(8,128)})) %all-reduce.6.cloned.1.call-update) | async-done | bytes 524304 | tf_op jit(solution)/shard_map/psum | solution.py:65
  922.5 1.7 add.33
  924.2 1.7 add.34
  (14 shorter events, 0.2 us)
Async XLA Ops:
  7.2 301.4 %copy-start = (bf16[1024,512]{1,0:T(8,128)(2,1)S(1)}, bf16[1024,512]{1,0:T(8,128)(2,1)}, u32[]{:S(2)}) copy-start(bf16[1024,512]{1,0:T(8,128)(2,1)} %param.7) | copy-start | bytes 3145732
  7.2 301.4 %all-reduce.4.cloned.1.call-start = ((), (), s32[]{:S(2)}) async-start(), calls=%async_computation.1 | async-start | bytes 2097152 | tf_op jit(solution)/shard_map/psum | solution.py:11
  97.1 363.4 %reduce-scatter.4.cloned.1.call-start = ((), (), s32[]{:S(2)}) async-start(), calls=%async_computation.2 | async-start | bytes 2162688
  312.2 610.3 %copy-start.1 = (f32[256,256]{1,0:T(8,128)S(1)}, f32[256,256]{1,0:T(8,128)}, u32[]{:S(2)}) copy-start(f32[256,256]{1,0:T(8,128)} %param.10) | copy-start | bytes 786436
  312.2 611.9 %copy-start.2 = (f32[256,256]{1,0:T(8,128)S(1)}, f32[256,256]{1,0:T(8,128)}, u32[]{:S(2)}) copy-start(f32[256,256]{1,0:T(8,128)} %param.11) | copy-start | bytes 786436
  312.3 610.2 %all-reduce.6.cloned.1.call-start = ((), (), s32[]{:S(2)}) async-start(), calls=%async_computation.3 | async-start | bytes 1048576 | tf_op jit(solution)/shard_map/psum | solution.py:65
Sparse Core Ops, SparseCore 0:
  97.2 211.3 all-reduce.3
  312.4 148.0 reduce-scatter.3
  466.6 455.8 all-reduce.5
where the time goes:
time: 933 us; the launch traced here: 932 us
  waiting for transfers between devices  816 us (87%)
  blocking collectives  85.3 us (9%)
  between operations  13.8 us (1%)
    psum x1, waiting for transfers between devices, per_device(): total_one, total_two = lax.psum((term_one, term_two), ('row', 'col'))  456 us
    psum x1, waiting for transfers between devices, broadcast(): return lax.psum(block, axis)  211 us
    unnamed x4, waiting for transfers between devices  148 us
    all_gather x1, blocking collectives, per_device(): lax.all_gather(masked_one, 'col', axis=0, tiled=True)  46 us
    all_gather x1, blocking collectives, per_device(): lax.all_gather(masked_two, 'col', axis=0, tiled=True)  39.3 us
  transfers between devices with their start and end apart: 3, of which 3 were waited for; matrix products, arithmetic and copies ran while one was open for 0% of the time, Pallas kernels for 0%

commit v1 on v0

--- a/solution.py
+++ b/solution.py
@@ -32,7 +32,9 @@
     masked_two = factor_two * mask_two.astype(jnp.bfloat16)[:, None]
     strip_one, strip_two = (
         lax.all_gather(masked_one, "col", axis=0, tiled=True),
-        lax.all_gather(masked_two, "col", axis=0, tiled=True),
+        jnp.concatenate(
+            lax.all_to_all(jnp.stack([masked_two] * lax.axis_size("col")), "col", 0, 0), axis=0
+        ),
     )
     stacked = jnp.concatenate([strip_one, strip_two], axis=1)
     col_ratio = num_col // num_row

time: 933 us -> 904 us (0.969)
  blocking collectives: 85.3 us -> 45.8 us
    all_gather x1 -> x0, blocking collectives: 39.3 us -> none  [per_device(): lax.all_gather(masked_two, 'col', axis=0, tiled=True)]
  transfers between devices with their start and end apart: 3 -> 4, of which waited for: 3 -> 3; matrix products, arithmetic and copies ran while one was open for 0% -> 0% of each run, Pallas kernels for 0% -> 0%
where the time goes in v1:
time: 904 us; the launch traced here: 903 us
  waiting for transfers between devices  816 us (90%)
  blocking collectives  45.8 us (5%)
  between operations  13.8 us (2%)
  starting transfers between devices  9.05 us (1%)
    psum x1, waiting for transfers between devices, per_device(): total_one, total_two = lax.psum((term_one, term_two), ('row', 'col'))  456 us
    psum x1, waiting for transfers between devices, broadcast(): return lax.psum(block, axis)  212 us
    unnamed x4, waiting for transfers between devices  148 us
    all_gather x1, blocking collectives, per_device(): lax.all_gather(masked_one, 'col', axis=0, tiled=True)  45.8 us
  transfers between devices with their start and end apart: 4, of which 3 were waited for; matrix products, arithmetic and copies ran while one was open for 0% of the time, Pallas kernels for 0%

profile of v1, /device:TPU:2, one launch (start us, length us, event | category | flops | bytes accessed | tf_op | source)
XLA Modules:
  0.0 903.3 jit_solution(11118887194067052338)
XLA Ops:
  7.2 0.8 broadcast_bitcast_fusion.1
  8.0 0.7 broadcast_bitcast_fusion
  8.8 0.1 dynamic-slice_convert_fusion
  8.9 0.8 broadcast_multiply_fusion
  9.7 0.9 stack.2
  10.6 8.9 all-to-all-start
  19.6 0.8 broadcast_multiply_fusion.1
  20.3 45.8 %all_gather.3 = bf16[1024,256]{1,0:T(8,128)(2,1)S(1)} all-gather(bf16[32,256]{1,0:T(8,128)(2,1)S(1)} %broadcast_multiply_fusion.1), channel_id=1, replica_groups=mesh['row'=16,'col'=32] {'col'}, dimensions={0}, use_global_device_ids=true | all-gather | bytes 540672 | tf_op jit(solution)/shard_map/all_gather | solution.py:34
  66.2 1.2 maximum_select_fusion
  67.4 0.0 reduce-scatter.4.cloned.1.call-start
  67.5 211.9 %all-reduce.4.cloned.1.call-done = bf16[1024,512]{1,0:T(8,128)(2,1)} async-done(((bf16[1024,512]{1,0:T(8,128)(2,1)}), bf16[1024,512]{1,0:T(8,128)(2,1)}) %all-reduce.4.cloned.1.call-update) | async-done | bytes 1048592 | tf_op jit(solution)/shard_map/psum | solution.py:11
  279.4 1.8 convolution_bitcast_fusion
  281.2 1.9 copy.15
  283.2 148.2 %reduce-scatter.4.cloned.1.call-done = f32[32,512]{1,0:T(8,128)} async-done(((f32[1024,512]{1,0:T(8,128)}), f32[32,512]{1,0:T(8,128)}) %reduce-scatter.4.cloned.1.call-update) | async-done | bytes 65552
  431.3 0.8 fusion.6
  432.1 0.1 copy.18
  432.2 1.8 fusion.2
  434.0 1.8 fusion.4
  435.8 0.7 copy.14
  436.5 0.1 copy.17
  436.6 0.7 copy.13
  437.3 456.1 %all-reduce.6.cloned.1.call-done = (f32[256,256]{1,0:T(8,128)}, f32[256,256]{1,0:T(8,128)}) async-done(((f32[256,256]{1,0:T(8,128)}, f32[256,256]{1,0:T(8,128)}), (f32[256,256]{1,0:T(8,128)}, f32[256,256]{1,0:T(8,128)})) %all-reduce.6.cloned.1.call-update) | async-done | bytes 524304 | tf_op jit(solution)/shard_map/psum | solution.py:67
  893.4 1.7 add.33
  895.1 1.7 add.34
  (16 shorter events, 0.3 us)
Async XLA Ops:
  7.2 272.3 %copy-start = (bf16[1024,512]{1,0:T(8,128)(2,1)S(1)}, bf16[1024,512]{1,0:T(8,128)(2,1)}, u32[]{:S(2)}) copy-start(bf16[1024,512]{1,0:T(8,128)(2,1)} %param.7) | copy-start | bytes 3145732
  10.6 55.6 %all-to-all-start = ((bf16[32,32,256]{2,1,0:T(8,128)(2,1)}), bf16[32,32,256]{2,1,0:T(8,128)(2,1)S(1)}, u32[]{:S(2)}, u32[]{:S(2)}) async-start(bf16[32,32,256]{2,1,0:T(8,128)(2,1)} %stack.2), calls=%async_computation | async-start | bytes 1048576 | tf_op jit(solution)/shard_map/all_to_all | solution.py:36
  19.5 259.9 %all-reduce.4.cloned.1.call-start = ((), (), s32[]{:S(2)}) async-start(), calls=%async_computation.2 | async-start | bytes 2097152 | tf_op jit(solution)/shard_map/psum | solution.py:11
  67.4 363.9 %reduce-scatter.4.cloned.1.call-start = ((), (), s32[]{:S(2)}) async-start(), calls=%async_computation.3 | async-start | bytes 2162688
  283.1 610.3 %copy-start.1 = (f32[256,256]{1,0:T(8,128)S(1)}, f32[256,256]{1,0:T(8,128)}, u32[]{:S(2)}) copy-start(f32[256,256]{1,0:T(8,128)} %param.10) | copy-start | bytes 786436
  283.1 612.0 %copy-start.2 = (f32[256,256]{1,0:T(8,128)S(1)}, f32[256,256]{1,0:T(8,128)}, u32[]{:S(2)}) copy-start(f32[256,256]{1,0:T(8,128)} %param.11) | copy-start | bytes 786436
  283.1 610.3 %all-reduce.6.cloned.1.call-start = ((), (), s32[]{:S(2)}) async-start(), calls=%async_computation.4 | async-start | bytes 1048576 | tf_op jit(solution)/shard_map/psum | solution.py:67
Sparse Core Ops, SparseCore 0:
  67.5 211.8 all-reduce.3
  283.2 148.0 reduce-scatter.3
  437.4 455.9 all-reduce.5

commit v2 on v0

--- a/solution.py
+++ b/solution.py
@@ -62,7 +62,7 @@
         precision=lax.Precision.HIGHEST,
         preferred_element_type=jnp.float32,
     )
-    total_one, total_two = lax.psum((term_one, term_two), ("row", "col"))
+    total_one, total_two = lax.psum(lax.psum((term_one, term_two), "col"), "row")
     return (column_one, column_two, diag_inv_one + total_one, diag_inv_two + total_two)
 
 

time: 933 us -> 967 us (1.036)
  the two profiles are of different devices: /device:TPU:2 before, /device:TPU:8 now
where the time goes in v2:
time: 967 us
  waiting for transfers between devices  850 us (88%)
  blocking collectives  85.4 us (9%)
  between operations  13.9 us (1%)
    psum x1, waiting for transfers between devices, per_device(): lax.psum((term_one, term_two), 'col')  284 us
    psum x1, waiting for transfers between devices, broadcast(): return lax.psum(block, axis)  214 us
    psum x1, waiting for transfers between devices, per_device(): lax.psum(lax.psum((term_one, term_two), 'col'), 'row')  212 us
    unnamed x5, waiting for transfers between devices  141 us
    all_gather x1, blocking collectives, per_device(): lax.all_gather(masked_one, 'col', axis=0, tiled=True)  44.8 us
    all_gather x1, blocking collectives, per_device(): lax.all_gather(masked_two, 'col', axis=0, tiled=True)  40.6 us
  transfers between devices with their start and end apart: 4, of which 4 were waited for; matrix products, arithmetic and copies ran while one was open for 0% of the time, Pallas kernels for 0%

profile of v2, /device:TPU:8, one launch (start us, length us, event | category | flops | bytes accessed | tf_op | source)
XLA Modules:
  0.0 966.8 jit_solution(10877625859708968709)
XLA Ops:
  7.2 0.8 broadcast_bitcast_fusion.1
  8.1 0.7 broadcast_bitcast_fusion
  8.9 0.1 dynamic-slice_convert_fusion
  8.9 0.8 broadcast_multiply_fusion.1
  9.7 44.8 %all_gather.6 = bf16[1024,256]{1,0:T(8,128)(2,1)S(1)} all-gather(bf16[32,256]{1,0:T(8,128)(2,1)S(1)} %broadcast_multiply_fusion.1), channel_id=1, replica_groups=mesh['row'=16,'col'=32] {'col'}, dimensions={0}, use_global_device_ids=true | all-gather | bytes 540672 | tf_op jit(solution)/shard_map/all_gather | solution.py:34
  54.5 0.8 broadcast_multiply_fusion
  55.3 40.6 %all_gather.7 = bf16[1024,256]{1,0:T(8,128)(2,1)S(1)} all-gather(bf16[32,256]{1,0:T(8,128)(2,1)S(1)} %broadcast_multiply_fusion), channel_id=1, replica_groups=mesh['row'=16,'col'=32] {'col'}, dimensions={0}, use_global_device_ids=true | all-gather | bytes 540672 | tf_op jit(solution)/shard_map/all_gather | solution.py:35
  95.9 1.2 maximum_select_fusion
  97.2 213.6 %all-reduce.6.cloned.1.call-done = bf16[1024,512]{1,0:T(8,128)(2,1)} async-done(((bf16[1024,512]{1,0:T(8,128)(2,1)}), bf16[1024,512]{1,0:T(8,128)(2,1)}) %all-reduce.6.cloned.1.call-update) | async-done | bytes 1048592 | tf_op jit(solution)/shard_map/psum | solution.py:11
  310.8 1.8 convolution_bitcast_fusion
  312.6 1.9 copy.15
  314.5 140.5 %reduce-scatter.4.cloned.1.call-done = f32[32,512]{1,0:T(8,128)} async-done(((f32[1024,512]{1,0:T(8,128)}), f32[32,512]{1,0:T(8,128)}) %reduce-scatter.4.cloned.1.call-update) | async-done | bytes 65552
  455.1 1.8 fusion.2
  456.9 1.8 fusion.4
  458.6 0.0 all-reduce.10.cloned.1.call-start
  458.7 284.2 %all-reduce.8.cloned.1.call-done = (f32[256,256]{1,0:T(8,128)}, f32[256,256]{1,0:T(8,128)}) async-done(((f32[256,256]{1,0:T(8,128)}, f32[256,256]{1,0:T(8,128)}), (f32[256,256]{1,0:T(8,128)}, f32[256,256]{1,0:T(8,128)})) %all-reduce.8.cloned.1.call-update) | async-done | bytes 524304 | tf_op jit(solution)/shard_map/psum | solution.py:65
  742.9 0.8 fusion.6
  743.7 0.1 copy.18
  743.8 0.7 copy.14
  744.5 0.1 copy.17
  744.6 0.7 copy.13
  745.3 211.6 %all-reduce.10.cloned.1.call-done = (f32[256,256]{1,0:T(8,128)}, f32[256,256]{1,0:T(8,128)}) async-done(((f32[256,256]{1,0:T(8,128)}, f32[256,256]{1,0:T(8,128)}), (f32[256,256]{1,0:T(8,128)}, f32[256,256]{1,0:T(8,128)})) %all-reduce.10.cloned.1.call-update) | async-done | bytes 524304 | tf_op jit(solution)/shard_map/psum | solution.py:65
  956.9 1.7 add.37
  958.6 1.7 add.38
  (17 shorter events, 0.3 us)
Async XLA Ops:
  7.2 303.6 %copy-start = (bf16[1024,512]{1,0:T(8,128)(2,1)S(1)}, bf16[1024,512]{1,0:T(8,128)(2,1)}, u32[]{:S(2)}) copy-start(bf16[1024,512]{1,0:T(8,128)(2,1)} %param.7) | copy-start | bytes 3145732
  7.2 303.6 %all-reduce.6.cloned.1.call-start = ((), (), s32[]{:S(2)}) async-start(), calls=%async_computation.1 | async-start | bytes 2097152 | tf_op jit(solution)/shard_map/psum | solution.py:11
  97.2 357.9 %reduce-scatter.4.cloned.1.call-start = ((), (), s32[]{:S(2)}) async-start(), calls=%async_computation.2 | async-start | bytes 2162688
  314.5 642.5 %copy-start.1 = (f32[256,256]{1,0:T(8,128)S(1)}, f32[256,256]{1,0:T(8,128)}, u32[]{:S(2)}) copy-start(f32[256,256]{1,0:T(8,128)} %param.10) | copy-start | bytes 786436
  314.5 644.1 %copy-start.2 = (f32[256,256]{1,0:T(8,128)S(1)}, f32[256,256]{1,0:T(8,128)}, u32[]{:S(2)}) copy-start(f32[256,256]{1,0:T(8,128)} %param.11) | copy-start | bytes 786436
  314.5 428.4 %all-reduce.8.cloned.1.call-start = ((), (), s32[]{:S(2)}) async-start(), calls=%async_computation.3 | async-start | bytes 1048576 | tf_op jit(solution)/shard_map/psum | solution.py:65
  458.6 498.3 %all-reduce.10.cloned.1.call-start = ((), (), s32[]{:S(2)}) async-start(), calls=%async_computation.4 | async-start | bytes 1048576 | tf_op jit(solution)/shard_map/psum | solution.py:65
Sparse Core Ops, SparseCore 0:
  97.3 213.4 all-reduce.5
  314.6 140.4 reduce-scatter.3
  458.8 284.0 all-reduce.7
  745.9 210.9 all-reduce.9

commit v3 on v0

--- a/solution.py
+++ b/solution.py
@@ -8,7 +8,7 @@
 
 def broadcast(block, axis, owner):
     block = jnp.where(lax.axis_index(axis) == owner, block, jnp.zeros_like(block))
-    return lax.psum(block, axis)
+    return jnp.sum(lax.all_gather(block, axis), axis=0)
 
 
 def local_mask(struct, first_row, row_count):

time: 933 us -> 1120 us (1.20)
  waiting for transfers between devices: 816 us -> 993 us
    all_gather x0 -> x1, waiting for transfers between devices: none -> 385 us  [broadcast(): return jnp.sum(lax.all_gather(block, axis), axis=0)]
    psum x1 -> x0, waiting for transfers between devices: 211 us -> none  [broadcast(): return lax.psum(block, axis)]
where the time goes in v3:
time: 1120 us
  waiting for transfers between devices  993 us (89%)
  blocking collectives  85.3 us (8%)
  other arithmetic  16.1 us (1%)
  between operations  13.8 us (1%)
    psum x1, waiting for transfers between devices, per_device(): total_one, total_two = lax.psum((term_one, term_two), ('row', 'col'))  456 us
    all_gather x1, waiting for transfers between devices, broadcast(): return jnp.sum(lax.all_gather(block, axis), axis=0)  385 us
    unnamed x4, waiting for transfers between devices  152 us
    all_gather x1, blocking collectives, per_device(): lax.all_gather(masked_one, 'col', axis=0, tiled=True)  46 us
    all_gather x1, blocking collectives, per_device(): lax.all_gather(masked_two, 'col', axis=0, tiled=True)  39.3 us
  transfers between devices with their start and end apart: 3, of which 3 were waited for; matrix products, arithmetic and copies ran while one was open for 0% of the time, Pallas kernels for 0%

profile of v3, /device:TPU:2, one launch (start us, length us, event | category | flops | bytes accessed | tf_op | source)
XLA Modules:
  0.0 1119.3 jit_solution(18106189279554462769)
XLA Ops:
  7.2 0.8 broadcast_bitcast_fusion.1
  8.1 0.7 broadcast_bitcast_fusion
  8.9 0.1 dynamic-slice_convert_fusion
  8.9 0.8 broadcast_multiply_fusion.1
  9.7 46.0 %all_gather.10 = bf16[1024,256]{1,0:T(8,128)(2,1)S(1)} all-gather(bf16[32,256]{1,0:T(8,128)(2,1)S(1)} %broadcast_multiply_fusion.1), channel_id=1, replica_groups=mesh['row'=16,'col'=32] {'col'}, dimensions={0}, use_global_device_ids=true | all-gather | bytes 540672 | tf_op jit(solution)/shard_map/all_gather | solution.py:34
  55.7 0.8 broadcast_multiply_fusion
  56.5 39.3 %all_gather.11 = bf16[1024,256]{1,0:T(8,128)(2,1)S(1)} all-gather(bf16[32,256]{1,0:T(8,128)(2,1)S(1)} %broadcast_multiply_fusion), channel_id=1, replica_groups=mesh['row'=16,'col'=32] {'col'}, dimensions={0}, use_global_device_ids=true | all-gather | bytes 540672 | tf_op jit(solution)/shard_map/all_gather | solution.py:35
  95.8 1.2 maximum_select_fusion
  97.0 0.0 reduce-scatter.4.cloned.1.call-start
  97.1 384.7 %all-gather.2.cloned.1.call-done = bf16[16,1024,512]{2,1,0:T(8,128)(2,1)} async-done(((bf16[1,1024,512]{2,1,0:T(8,128)(2,1)}), bf16[16,1024,512]{2,1,0:T(8,128)(2,1)}) %all-gather.2.cloned.1.call-update) | async-done | bytes 16777232 | tf_op jit(solution)/shard_map/all_gather | solution.py:11
  481.8 9.9 reduce_sum.12
  491.7 1.8 convolution_bitcast_fusion
  493.5 1.9 copy.15
  495.5 152.0 %reduce-scatter.4.cloned.1.call-done = f32[32,512]{1,0:T(8,128)} async-done(((f32[1024,512]{1,0:T(8,128)}), f32[32,512]{1,0:T(8,128)}) %reduce-scatter.4.cloned.1.call-update) | async-done | bytes 65552
  647.4 0.8 fusion.6
  648.2 0.1 copy.18
  648.3 1.8 fusion.2
  650.1 1.8 fusion.4
  651.9 0.7 copy.14
  652.6 0.1 copy.17
  652.7 0.7 copy.13
  653.4 456.0 %all-reduce.3.cloned.1.call-done = (f32[256,256]{1,0:T(8,128)}, f32[256,256]{1,0:T(8,128)}) async-done(((f32[256,256]{1,0:T(8,128)}, f32[256,256]{1,0:T(8,128)}), (f32[256,256]{1,0:T(8,128)}, f32[256,256]{1,0:T(8,128)})) %all-reduce.3.cloned.1.call-update) | async-done | bytes 524304 | tf_op jit(solution)/shard_map/psum | solution.py:65
  1109.4 1.7 add.31
  1111.1 1.7 add.32
  (15 shorter events, 0.3 us)
Async XLA Ops:
  7.2 484.5 %copy-start = (bf16[1024,512]{1,0:T(8,128)(2,1)S(1)}, bf16[1024,512]{1,0:T(8,128)(2,1)}, u32[]{:S(2)}) copy-start(bf16[1024,512]{1,0:T(8,128)(2,1)} %param.7) | copy-start | bytes 3145732
  7.2 474.6 %all-gather.2.cloned.1.call-start = ((), (), s32[]{:S(2)}) async-start(), calls=%async_computation.1 | async-start | bytes 17825792 | tf_op jit(solution)/shard_map/all_gather | solution.py:11
  97.0 550.4 %reduce-scatter.4.cloned.1.call-start = ((), (), s32[]{:S(2)}) async-start(), calls=%async_computation.2 | async-start | bytes 2162688
  495.4 614.0 %copy-start.1 = (f32[256,256]{1,0:T(8,128)S(1)}, f32[256,256]{1,0:T(8,128)}, u32[]{:S(2)}) copy-start(f32[256,256]{1,0:T(8,128)} %param.10) | copy-start | bytes 786436
  495.4 615.7 %copy-start.2 = (f32[256,256]{1,0:T(8,128)S(1)}, f32[256,256]{1,0:T(8,128)}, u32[]{:S(2)}) copy-start(f32[256,256]{1,0:T(8,128)} %param.11) | copy-start | bytes 786436
  495.4 614.0 %all-reduce.3.cloned.1.call-start = ((), (), s32[]{:S(2)}) async-start(), calls=%async_computation.3 | async-start | bytes 1048576 | tf_op jit(solution)/shard_map/psum | solution.py:65
Sparse Core Ops, SparseCore 0:
  97.1 384.6 all-gather.1
  495.5 151.8 reduce-scatter.3
  654.4 454.9 all-reduce.2
